TPU v7x, 32 devices: a whole 2x2x4 slice. The times are simulated.
32 devices in a mesh: domain: 2 (over x), fsdp: 16 (over z, y, core).
Axes of the slice: x: 2, y: 2, z: 4, core: 2. Of those that a mesh axis runs over, the one named last changes fastest.
Arguments:
- gradients: bfloat16 [2, 4, 4096, 512], P('domain', None, 'fsdp')
- row_counts: int32 [4], replicated, may hold values from 2048 to 4096, as said below
- domain_ids: int32 [2], replicated, may hold values from 0 to 7
- domain_weights: float32 [8], replicated, may hold values from 0.2 to 2
Outputs:
- updates: float32 [4, 4096, 512], P('domain', 'fsdp')
- new_weights: float32 [8], replicated
Inputs may be any that keep to these rules, and one draw needn't show every extreme that they name: `row_counts`: each matrix has 4096 or 2048 rows, and both counts occur.
All inputs are finite; a program needn't handle non-finite values.
Results may differ from a plain program's by a relative error of at most 0.0071.
Values may be sent and summed in bfloat16 or wider, within the bound.
No kernel may reach another device: no remote copies, remote signals or barrier semaphores. Data moves between devices by JAX's collectives and lax.ppermute only.
A program may use at most 64 MiB of HBM per device.

v0:
```python
import math
import jax
import jax.numpy as jnp
from jax import lax
from jax.sharding import PartitionSpec as P

NS_ITERS = 3
OWNERS = 8
COEF_A = 3.4445
COEF_B = -4.775
COEF_C = 2.0315
MUON_SCALE = 0.2
ETA = 4.0


def partner(shard, axis, stride):
    return lax.ppermute(shard, axis, [(i, i ^ 1 << stride) for i in range(lax.axis_size(axis))])


def group_mixing(domain_ids, domain_weights, kind_count):
    weight_share = domain_weights / jnp.sum(domain_weights)
    onehot = (domain_ids[:, None] == jnp.arange(kind_count, dtype=jnp.int32)[None, :]).astype(
        jnp.float32
    )
    counts = jnp.sum(onehot, axis=0)
    per_member = weight_share / jnp.maximum(counts, 1.0)
    group_mix = jnp.sum(onehot * per_member[None, :], axis=1)
    return (weight_share, onehot, counts, group_mix)


def summed_gram(iterate):
    gram_total = lax.dot_general(
        iterate, iterate, (((0,), (0,)), ((), ())), preferred_element_type=jnp.float32
    )
    for bit_pos in range(OWNERS.bit_length() - 1):
        gram_total = gram_total + partner(gram_total, "fsdp", bit_pos)
    return gram_total


def newton_steps(iterate):
    for repeat in range(NS_ITERS):
        gram_full = lax.optimization_barrier(summed_gram(iterate).astype(jnp.bfloat16))
        square = jnp.dot(gram_full, gram_full, preferred_element_type=jnp.float32)
        poly_term = (COEF_B * gram_full.astype(jnp.float32) + COEF_C * square).astype(jnp.bfloat16)
        iterate = lax.optimization_barrier(
            (
                COEF_A * iterate.astype(jnp.float32)
                + jnp.dot(iterate, poly_term, preferred_element_type=jnp.float32)
            ).astype(jnp.bfloat16)
        )
    return iterate


def share_scores(aligned, squares, norm_slots):
    return lax.psum((aligned, squares, norm_slots), ("domain", "fsdp"))


def body(gradients, row_counts, domain_ids, domain_weights):
    groups = lax.axis_size("domain")
    shards = lax.axis_size("fsdp")
    matrices = row_counts.shape[0]
    rows_src = gradients.shape[2]
    columns = gradients.shape[3]
    per_domain = matrices // groups
    sub_rows = rows_src // OWNERS
    own_rows = shards * sub_rows
    full_rows = rows_src * shards
    domain_pos = lax.axis_index("domain")
    shard_pos = lax.axis_index("fsdp")
    weight_share, onehot, counts, group_mix = group_mixing(
        domain_ids, domain_weights, domain_weights.shape[0]
    )
    blocks = lax.all_to_all(
        gradients.reshape(1, groups, per_domain, rows_src, columns),
        "domain",
        split_axis=1,
        concat_axis=0,
        tiled=True,
    )
    blocks = blocks.reshape(groups, per_domain, rows_src, columns)
    global_rows = shard_pos * rows_src + jnp.arange(rows_src, dtype=jnp.int32)
    limits = lax.dynamic_slice_in_dim(row_counts, domain_pos * per_domain, per_domain, 0)
    row_mask = (global_rows[None, :] < limits[:, None])[None, :, :, None]
    masked = jnp.where(row_mask, blocks.astype(jnp.float32), jnp.zeros((), jnp.float32))
    combined = jnp.sum(group_mix[:, None, None, None] * masked, axis=0)
    aligned = jnp.sum(masked * combined[None], axis=(1, 2, 3))
    squares = jnp.sum(masked * masked, axis=(1, 2, 3))
    block_squares = jnp.sum(combined * combined, axis=(1, 2))
    norm_slots = lax.dynamic_update_slice_in_dim(
        jnp.zeros((matrices,), jnp.float32), block_squares, domain_pos * per_domain, 0
    )
    aligned, squares, norm_slots = share_scores(aligned, squares, norm_slots)
    frob_norm = (
        jnp.sqrt(lax.dynamic_slice_in_dim(norm_slots, domain_pos * per_domain, per_domain, 0))
        + 1e-07
    )
    scaled = (combined / frob_norm[:, None, None]).astype(jnp.bfloat16)
    scaled = scaled.reshape(shards, 1, sub_rows, columns)
    start_rows = lax.all_to_all(scaled, "fsdp", split_axis=0, concat_axis=1, tiled=True)
    start_rows = lax.optimization_barrier(start_rows.reshape(own_rows, columns))
    finished = newton_steps(start_rows)
    returned = lax.all_to_all(
        finished.reshape(1, shards, sub_rows, columns),
        "fsdp",
        split_axis=1,
        concat_axis=0,
        tiled=True,
    )
    returned = returned.reshape(per_domain, rows_src, columns)
    updates = returned.astype(jnp.float32) * (MUON_SCALE * math.sqrt(full_rows))
    total_sq = jnp.sum(norm_slots)
    cosine = aligned / (jnp.sqrt(squares) * jnp.sqrt(total_sq) + 1e-06)
    score = jnp.sum(onehot * cosine[:, None], axis=0) / jnp.maximum(counts, 1.0)
    raised = weight_share * jnp.exp(ETA * score)
    return (updates, raised / jnp.sum(raised))


def solution(mesh):
    placed = (P("domain", None, "fsdp", None), P(), P(), P())
    return jax.shard_map(
        body,
        mesh=mesh,
        in_specs=placed,
        out_specs=(P("domain", "fsdp", None), P()),
        check_vma=False,
    )
```

profile of v0, /device:TPU:0, one launch (start us, length us, event | category | flops | bytes accessed | tf_op | source)
XLA Modules:
  0.0 265.7 jit_solution(6877497156156330844)
XLA Ops:
  0.7 4.4 %all-to-all-start = ((bf16[1,2,2,256,512]{4,3,2,0,1:T(8,128)(2,1)}), bf16[1,2,2,256,512]{4,3,2,0,1:T(8,128)(2,1)S(1)}, u32[]{:S(2)}, u32[]{:S(2)}) async-start(bf16[1,2,2,256,512]{4,3,2,0,1:T(8,128)(2,1)} %bitcast.31), calls=%async_computation | async-start | bytes 2097152 | tf_op jit(solution)/shard_map/all_to_all | solution.py:73
  6.7 12.7 %all-to-all-done = bf16[1,2,2,256,512]{4,3,2,0,1:T(8,128)(2,1)S(1)} async-done(((bf16[1,2,2,256,512]{4,3,2,0,1:T(8,128)(2,1)}), bf16[1,2,2,256,512]{4,3,2,0,1:T(8,128)(2,1)S(1)}, u32[]{:S(2)}, u32[]{:S(2)}) %all-to-all-start) | async-done | bytes 1048608 | tf_op jit(solution)/shard_map/all_to_all | solution.py:73
  20.9 39.8 %all-reduce = (f32[4]{0:T(128)S(1)}, f32[2]{0:T(128)S(1)}, f32[2]{0:T(128)S(1)}) all-reduce(f32[4]{0:T(128)S(1)} %dynamic_update_slice.3, f32[2]{0:T(128)S(1)} %get-tuple-element.3, f32[2]{0:T(128)S(1)} %get-tuple-element.2), channel_id=1, replica_groups=mesh['domain'=2,'fsdp'=16] {'domain','fsdp'}, use_global_device_ids=true, to_apply=%region_5.6 | all-reduce | flops 8 | bytes 64 | tf_op jit(solution)/shard_map/psum | solution.py:55
  62.4 19.5 %all_to_all.12 = bf16[16,1,32,512]{3,2,1,0:T(8,128)(2,1)S(1)} all-to-all(bf16[16,1,32,512]{3,2,1,0:T(8,128)(2,1)S(1)} %divide_convert_fusion), channel_id=1, replica_groups=mesh['domain'=2,'fsdp'=16] {'fsdp'}, dimensions={0} | all-to-all | bytes 1048576 | tf_op jit(solution)/shard_map/all_to_all | solution.py:99
  82.6 2.5 collective-permute-done
  86.4 24.2 %collective-permute-done.1 = f32[512,512]{1,0:T(8,128)S(1)} collective-permute-done((f32[512,512]{1,0:T(8,128)S(1)}, f32[512,512]{1,0:T(8,128)S(1)}, u32[]{:S(2)}, u32[]{:S(2)}) %collective-permute-start.1) | collective-permute-done | bytes 1048608 | tf_op jit(solution)/shard_map/ppermute | solution.py:17
  110.8 1.8 collective-permute-start.2
  112.6 22.8 %collective-permute-done.2 = f32[512,512]{1,0:T(8,128)S(1)} collective-permute-done((f32[512,512]{1,0:T(8,128)S(1)}, f32[512,512]{1,0:T(8,128)S(1)}, u32[]{:S(2)}, u32[]{:S(2)}) %collective-permute-start.2) | collective-permute-done | bytes 1048608 | tf_op jit(solution)/shard_map/ppermute | solution.py:17
  137.0 2.6 collective-permute-done.3
  139.9 1.3 collective-permute-start.4
  141.2 23.9 %collective-permute-done.4 = f32[512,512]{1,0:T(8,128)S(1)} collective-permute-done((f32[512,512]{1,0:T(8,128)S(1)}, f32[512,512]{1,0:T(8,128)S(1)}, u32[]{:S(2)}, u32[]{:S(2)}) %collective-permute-start.4) | collective-permute-done | bytes 1048608 | tf_op jit(solution)/shard_map/ppermute | solution.py:17
  165.4 1.8 collective-permute-start.5
  167.2 22.6 %collective-permute-done.5 = f32[512,512]{1,0:T(8,128)S(1)} collective-permute-done((f32[512,512]{1,0:T(8,128)S(1)}, f32[512,512]{1,0:T(8,128)S(1)}, u32[]{:S(2)}, u32[]{:S(2)}) %collective-permute-start.5) | collective-permute-done | bytes 1048608 | tf_op jit(solution)/shard_map/ppermute | solution.py:17
  191.4 2.6 collective-permute-done.6
  194.2 1.3 collective-permute-start.7
  195.6 23.9 %collective-permute-done.7 = f32[512,512]{1,0:T(8,128)S(1)} collective-permute-done((f32[512,512]{1,0:T(8,128)S(1)}, f32[512,512]{1,0:T(8,128)S(1)}, u32[]{:S(2)}, u32[]{:S(2)}) %collective-permute-start.7) | collective-permute-done | bytes 1048608 | tf_op jit(solution)/shard_map/ppermute | solution.py:17
  219.7 1.8 collective-permute-start.8
  221.5 22.6 %collective-permute-done.8 = f32[512,512]{1,0:T(8,128)S(1)} collective-permute-done((f32[512,512]{1,0:T(8,128)S(1)}, f32[512,512]{1,0:T(8,128)S(1)}, u32[]{:S(2)}, u32[]{:S(2)}) %collective-permute-start.8) | collective-permute-done | bytes 1048608 | tf_op jit(solution)/shard_map/ppermute | solution.py:17
  244.4 1.6 fusion.8
  245.9 4.4 %all-to-all-start.2 = ((bf16[1,16,32,512]{3,2,0,1:T(8,128)(2,1)}), bf16[1,16,32,512]{3,2,0,1:T(8,128)(2,1)S(1)}, u32[]{:S(2)}, u32[]{:S(2)}) async-start(bf16[1,16,32,512]{3,2,0,1:T(8,128)(2,1)} %bitcast.5), calls=%async_computation.2 | async-start | bytes 1048576 | tf_op jit(solution)/shard_map/all_to_all | solution.py:102
  250.4 1.3 fusion.21
  251.8 1.2 broadcast_divide_fusion
  253.0 11.6 %all-to-all-done.2 = bf16[1,16,32,512]{3,2,0,1:T(8,128)(2,1)S(1)} async-done(((bf16[1,16,32,512]{3,2,0,1:T(8,128)(2,1)}), bf16[1,16,32,512]{3,2,0,1:T(8,128)(2,1)S(1)}, u32[]{:S(2)}, u32[]{:S(2)}) %all-to-all-start.2) | async-done | bytes 524320 | tf_op jit(solution)/shard_map/all_to_all | solution.py:102
  264.6 1.1 convert_multiply_fusion
  (42 shorter events, 10.6 us)
Async XLA Ops:
  0.6 4.4 %copy-start.2 = (s32[2]{0:T(128)S(1)}, s32[2]{0:T(128)}, u32[]{:S(2)}) copy-start(s32[2]{0:T(128)} %param.6) | copy-start | bytes 28
  0.6 4.5 %copy-start = (f32[8]{0:T(128)S(1)}, f32[8]{0:T(128)}, u32[]{:S(2)}) copy-start(f32[8]{0:T(128)} %param.7) | copy-start | bytes 100
  0.7 5.1 %copy-start.1 = (s32[4]{0:T(128)S(1)}, s32[4]{0:T(128)}, u32[]{:S(2)}) copy-start(s32[4]{0:T(128)} %param.5) | copy-start | bytes 52
  0.7 18.8 %all-to-all-start = ((bf16[1,2,2,256,512]{4,3,2,0,1:T(8,128)(2,1)}), bf16[1,2,2,256,512]{4,3,2,0,1:T(8,128)(2,1)S(1)}, u32[]{:S(2)}, u32[]{:S(2)}) async-start(bf16[1,2,2,256,512]{4,3,2,0,1:T(8,128)(2,1)} %bitcast.31), calls=%async_computation | async-start | bytes 2097152 | tf_op jit(solution)/shard_map/all_to_all | solution.py:73
  82.4 2.7 %collective-permute-start = (f32[512,512]{1,0:T(8,128)S(1)}, f32[512,512]{1,0:T(8,128)S(1)}, u32[]{:S(2)}, u32[]{:S(2)}) collective-permute-start(f32[512,512]{1,0:T(8,128)S(1)} %fusion.22), channel_id=1, source_target_pairs={{0,1},{1,0},{2,3},{3,2},{4,5},{5,4},{6,7},{7,6},{8,9},{9,8},{10,11... | collective-permute-start | bytes 3145736 | tf_op jit(solution)/shard_map/ppermute | solution.py:17
  85.3 25.3 %collective-permute-start.1 = (f32[512,512]{1,0:T(8,128)S(1)}, f32[512,512]{1,0:T(8,128)S(1)}, u32[]{:S(2)}, u32[]{:S(2)}) collective-permute-start(f32[512,512]{1,0:T(8,128)S(1)} %add.76), channel_id=1, source_target_pairs={{0,2},{1,3},{2,0},{3,1},{4,6},{5,7},{6,4},{7,5},{8,10},{9,11},{10,... | collective-permute-start | bytes 3145736 | tf_op jit(solution)/shard_map/ppermute | solution.py:17
  110.8 24.7 %collective-permute-start.2 = (f32[512,512]{1,0:T(8,128)S(1)}, f32[512,512]{1,0:T(8,128)S(1)}, u32[]{:S(2)}, u32[]{:S(2)}) collective-permute-start(f32[512,512]{1,0:T(8,128)S(1)} %add.77), channel_id=1, source_target_pairs={{0,4},{1,5},{2,6},{3,7},{4,0},{5,1},{6,2},{7,3},{8,12},{9,13},{10,... | collective-permute-start | bytes 3145736 | tf_op jit(solution)/shard_map/ppermute | solution.py:17
  137.0 2.7 %collective-permute-start.3 = (f32[512,512]{1,0:T(8,128)S(1)}, f32[512,512]{1,0:T(8,128)S(1)}, u32[]{:S(2)}, u32[]{:S(2)}) collective-permute-start(f32[512,512]{1,0:T(8,128)S(1)} %fusion.23), channel_id=1, source_target_pairs={{0,1},{1,0},{2,3},{3,2},{4,5},{5,4},{6,7},{7,6},{8,9},{9,8},{10,11... | collective-permute-start | bytes 3145736 | tf_op jit(solution)/shard_map/ppermute | solution.py:17
  139.9 25.3 %collective-permute-start.4 = (f32[512,512]{1,0:T(8,128)S(1)}, f32[512,512]{1,0:T(8,128)S(1)}, u32[]{:S(2)}, u32[]{:S(2)}) collective-permute-start(f32[512,512]{1,0:T(8,128)S(1)} %add.81), channel_id=1, source_target_pairs={{0,2},{1,3},{2,0},{3,1},{4,6},{5,7},{6,4},{7,5},{8,10},{9,11},{10,... | collective-permute-start | bytes 3145736 | tf_op jit(solution)/shard_map/ppermute | solution.py:17
  165.4 24.4 %collective-permute-start.5 = (f32[512,512]{1,0:T(8,128)S(1)}, f32[512,512]{1,0:T(8,128)S(1)}, u32[]{:S(2)}, u32[]{:S(2)}) collective-permute-start(f32[512,512]{1,0:T(8,128)S(1)} %add.82), channel_id=1, source_target_pairs={{0,4},{1,5},{2,6},{3,7},{4,0},{5,1},{6,2},{7,3},{8,12},{9,13},{10,... | collective-permute-start | bytes 3145736 | tf_op jit(solution)/shard_map/ppermute | solution.py:17
  191.3 2.7 %collective-permute-start.6 = (f32[512,512]{1,0:T(8,128)S(1)}, f32[512,512]{1,0:T(8,128)S(1)}, u32[]{:S(2)}, u32[]{:S(2)}) collective-permute-start(f32[512,512]{1,0:T(8,128)S(1)} %fusion.24), channel_id=1, source_target_pairs={{0,1},{1,0},{2,3},{3,2},{4,5},{5,4},{6,7},{7,6},{8,9},{9,8},{10,11... | collective-permute-start | bytes 3145736 | tf_op jit(solution)/shard_map/ppermute | solution.py:17
  194.2 25.3 %collective-permute-start.7 = (f32[512,512]{1,0:T(8,128)S(1)}, f32[512,512]{1,0:T(8,128)S(1)}, u32[]{:S(2)}, u32[]{:S(2)}) collective-permute-start(f32[512,512]{1,0:T(8,128)S(1)} %add.86), channel_id=1, source_target_pairs={{0,2},{1,3},{2,0},{3,1},{4,6},{5,7},{6,4},{7,5},{8,10},{9,11},{10,... | collective-permute-start | bytes 3145736 | tf_op jit(solution)/shard_map/ppermute | solution.py:17
  219.7 24.4 %collective-permute-start.8 = (f32[512,512]{1,0:T(8,128)S(1)}, f32[512,512]{1,0:T(8,128)S(1)}, u32[]{:S(2)}, u32[]{:S(2)}) collective-permute-start(f32[512,512]{1,0:T(8,128)S(1)} %add.87), channel_id=1, source_target_pairs={{0,4},{1,5},{2,6},{3,7},{4,0},{5,1},{6,2},{7,3},{8,12},{9,13},{10,... | collective-permute-start | bytes 3145736 | tf_op jit(solution)/shard_map/ppermute | solution.py:17
  245.9 18.7 %all-to-all-start.2 = ((bf16[1,16,32,512]{3,2,0,1:T(8,128)(2,1)}), bf16[1,16,32,512]{3,2,0,1:T(8,128)(2,1)S(1)}, u32[]{:S(2)}, u32[]{:S(2)}) async-start(bf16[1,16,32,512]{3,2,0,1:T(8,128)(2,1)} %bitcast.5), calls=%async_computation.2 | async-start | bytes 1048576 | tf_op jit(solution)/shard_map/all_to_all | solution.py:102
where the time goes:
time: 266 us
  waiting for transfers between devices  172 us (65%)
  blocking collectives  59.3 us (22%)
  starting transfers between devices  18.3 us (7%)
  other arithmetic  9.43 us (4%)
  matrix products  4.55 us (2%)
    ppermute x9, waiting for transfers between devices, partner(): lax.ppermute(shard, axis, [(i, i ^ 1 << stride) for i in range(lax.axis_s...  148 us
    psum x1, blocking collectives, share_scores(): return lax.psum((aligned, squares, norm_slots), ('domain', 'fsdp'))  39.8 us
    all_to_all x1, blocking collectives, body(): lax.all_to_all(scaled, 'fsdp', split_axis=0, concat_axis=1, tiled=True)  19.5 us
    all_to_all x1, waiting for transfers between devices, body(): lax.all_to_all(gradients.reshape(1, groups, per_domain, rows_src, columns...  12.7 us
    all_to_all x1, waiting for transfers between devices, body(): lax.all_to_all(finished.reshape(1, shards, sub_rows, columns), 'fsdp', sp...  11.6 us
    ppermute x9, starting transfers between devices, partner(): lax.ppermute(shard, axis, [(i, i ^ 1 << stride) for i in range(lax.axis_s...  9.5 us
  transfers between devices with their start and end apart: 11, of which 11 were waited for; matrix products, arithmetic and copies ran while one was open for 2% of the time, Pallas kernels for 0%

commit v1 on v0

--- a/solution.py
+++ b/solution.py
@@ -11,6 +11,17 @@
 COEF_C = 2.0315
 MUON_SCALE = 0.2
 ETA = 4.0
+
+
+def in_blocks(value, dim, size):
+    before, after = (value.shape[:dim], value.shape[dim + 1 :])
+    return jnp.moveaxis(value.reshape(*before, size, -1, *after), dim, 0)
+
+
+def joined_along(blocks, dim):
+    dims = list(blocks.shape[1:])
+    dims[dim] *= blocks.shape[0]
+    return jnp.moveaxis(blocks, 0, dim).reshape(dims)
 
 
 def partner(shard, axis, stride):
@@ -99,13 +110,17 @@
     start_rows = lax.all_to_all(scaled, "fsdp", split_axis=0, concat_axis=1, tiled=True)
     start_rows = lax.optimization_barrier(start_rows.reshape(own_rows, columns))
     finished = newton_steps(start_rows)
-    returned = lax.all_to_all(
-        finished.reshape(1, shards, sub_rows, columns),
-        "fsdp",
-        split_axis=1,
-        concat_axis=0,
-        tiled=True,
-    )
+    x = finished.reshape(1, shards, sub_rows, columns)
+    peers, mine = (lax.axis_size("fsdp"), lax.axis_index("fsdp"))
+    parts = in_blocks(x, 1, peers)
+    outs = [parts[mine]]
+    for step in range(1, peers):
+        sent = parts[(mine + step) % peers]
+        outs.append(
+            lax.ppermute(sent, "fsdp", [(i_2, (i_2 + step) % peers) for i_2 in range(peers)])
+        )
+    parts = jnp.stack(outs)[(mine - jnp.arange(peers)) % peers]
+    returned = joined_along(parts, 0)
     returned = returned.reshape(per_domain, rows_src, columns)
     updates = returned.astype(jnp.float32) * (MUON_SCALE * math.sqrt(full_rows))
     total_sq = jnp.sum(norm_slots)

time: 266 us -> 272 us (1.023)
  starting transfers between devices: 18.3 us -> 35.4 us
  waiting for transfers between devices: 172 us -> 162 us
    ppermute x0 -> x15, starting transfers between devices: none -> 21.5 us  [body(): lax.ppermute(sent, 'fsdp', [(i_2, (i_2 + step) % peers) for i_2 in range(...]
    all_to_all x1 -> x0, waiting for transfers between devices: 11.6 us -> none  [body(): lax.all_to_all(finished.reshape(1, shards, sub_rows, columns), 'fsdp', sp...]
    all_to_all x1 -> x0, starting transfers between devices: 4.4 us -> none  [body(): lax.all_to_all(finished.reshape(1, shards, sub_rows, columns), 'fsdp', sp...]
  transfers between devices with their start and end apart: 11 -> 25, of which waited for: 11 -> 12; matrix products, arithmetic and copies ran while one was open for 2% -> 2% of each run, Pallas kernels for 0% -> 0%
where the time goes in v1:
time: 272 us
  waiting for transfers between devices  162 us (60%)
  blocking collectives  59.3 us (22%)
  starting transfers between devices  35.4 us (13%)
  other arithmetic  9.32 us (3%)
  matrix products  3.76 us (1%)
    ppermute x9, waiting for transfers between devices, partner(): lax.ppermute(shard, axis, [(i, i ^ 1 << stride) for i in range(lax.axis_s...  147 us
    psum x1, blocking collectives, share_scores(): return lax.psum((aligned, squares, norm_slots), ('domain', 'fsdp'))  39.8 us
    ppermute x15, starting transfers between devices, body(): lax.ppermute(sent, 'fsdp', [(i_2, (i_2 + step) % peers) for i_2 in range(...  21.5 us
    all_to_all x1, blocking collectives, body(): lax.all_to_all(scaled, 'fsdp', split_axis=0, concat_axis=1, tiled=True)  19.5 us
    all_to_all x1, waiting for transfers between devices, body(): lax.all_to_all(gradients.reshape(1, groups, per_domain, rows_src, columns...  12.7 us
    ppermute x9, starting transfers between devices, partner(): lax.ppermute(shard, axis, [(i, i ^ 1 << stride) for i in range(lax.axis_s...  9.47 us
  transfers between devices with their start and end apart: 25, of which 12 were waited for; matrix products, arithmetic and copies ran while one was open for 2% of the time, Pallas kernels for 0%

profile of v1, /device:TPU:0, one launch (start us, length us, event | category | flops | bytes accessed | tf_op | source)
XLA Modules:
  0.0 272.1 jit_solution(4355042236437863641)
XLA Ops:
  0.7 4.4 %all-to-all-start = ((bf16[1,2,2,256,512]{4,3,2,0,1:T(8,128)(2,1)}), bf16[1,2,2,256,512]{4,3,2,0,1:T(8,128)(2,1)S(1)}, u32[]{:S(2)}, u32[]{:S(2)}) async-start(bf16[1,2,2,256,512]{4,3,2,0,1:T(8,128)(2,1)} %bitcast.92), calls=%async_computation | async-start | bytes 2097152 | tf_op jit(solution)/shard_map/all_to_all | solution.py:84
  6.7 12.7 %all-to-all-done = bf16[1,2,2,256,512]{4,3,2,0,1:T(8,128)(2,1)S(1)} async-done(((bf16[1,2,2,256,512]{4,3,2,0,1:T(8,128)(2,1)}), bf16[1,2,2,256,512]{4,3,2,0,1:T(8,128)(2,1)S(1)}, u32[]{:S(2)}, u32[]{:S(2)}) %all-to-all-start) | async-done | bytes 1048608 | tf_op jit(solution)/shard_map/all_to_all | solution.py:84
  20.9 39.8 %all-reduce = (f32[4]{0:T(128)S(1)}, f32[2]{0:T(128)S(1)}, f32[2]{0:T(128)S(1)}) all-reduce(f32[4]{0:T(128)S(1)} %dynamic_update_slice.3, f32[2]{0:T(128)S(1)} %get-tuple-element.3, f32[2]{0:T(128)S(1)} %get-tuple-element.2), channel_id=1, replica_groups=mesh['domain'=2,'fsdp'=16] {'domain','fsdp'}, use_global_device_ids=true, to_apply=%region_5.6 | all-reduce | flops 8 | bytes 64 | tf_op jit(solution)/shard_map/psum | solution.py:66
  62.4 19.5 %all_to_all.8 = bf16[16,1,32,512]{3,2,1,0:T(8,128)(2,1)S(1)} all-to-all(bf16[16,1,32,512]{3,2,1,0:T(8,128)(2,1)S(1)} %divide_convert_fusion), channel_id=1, replica_groups=mesh['domain'=2,'fsdp'=16] {'fsdp'}, dimensions={0} | all-to-all | bytes 1048576 | tf_op jit(solution)/shard_map/all_to_all | solution.py:110
  82.6 2.5 collective-permute-done
  86.4 24.2 %collective-permute-done.1 = f32[512,512]{1,0:T(8,128)S(1)} collective-permute-done((f32[512,512]{1,0:T(8,128)S(1)}, f32[512,512]{1,0:T(8,128)S(1)}, u32[]{:S(2)}, u32[]{:S(2)}) %collective-permute-start.1) | collective-permute-done | bytes 1048608 | tf_op jit(solution)/shard_map/ppermute | solution.py:28
  110.8 1.8 collective-permute-start.2
  112.6 22.8 %collective-permute-done.2 = f32[512,512]{1,0:T(8,128)S(1)} collective-permute-done((f32[512,512]{1,0:T(8,128)S(1)}, f32[512,512]{1,0:T(8,128)S(1)}, u32[]{:S(2)}, u32[]{:S(2)}) %collective-permute-start.2) | collective-permute-done | bytes 1048608 | tf_op jit(solution)/shard_map/ppermute | solution.py:28
  137.0 2.6 collective-permute-done.3
  141.2 24.0 %collective-permute-done.4 = f32[512,512]{1,0:T(8,128)S(1)} collective-permute-done((f32[512,512]{1,0:T(8,128)S(1)}, f32[512,512]{1,0:T(8,128)S(1)}, u32[]{:S(2)}, u32[]{:S(2)}) %collective-permute-start.4) | collective-permute-done | bytes 1048608 | tf_op jit(solution)/shard_map/ppermute | solution.py:28
  165.4 1.8 collective-permute-start.5
  167.2 22.6 %collective-permute-done.5 = f32[512,512]{1,0:T(8,128)S(1)} collective-permute-done((f32[512,512]{1,0:T(8,128)S(1)}, f32[512,512]{1,0:T(8,128)S(1)}, u32[]{:S(2)}, u32[]{:S(2)}) %collective-permute-start.5) | collective-permute-done | bytes 1048608 | tf_op jit(solution)/shard_map/ppermute | solution.py:28
  191.4 2.6 collective-permute-done.6
  195.5 24.0 %collective-permute-done.7 = f32[512,512]{1,0:T(8,128)S(1)} collective-permute-done((f32[512,512]{1,0:T(8,128)S(1)}, f32[512,512]{1,0:T(8,128)S(1)}, u32[]{:S(2)}, u32[]{:S(2)}) %collective-permute-start.7) | collective-permute-done | bytes 1048608 | tf_op jit(solution)/shard_map/ppermute | solution.py:28
  219.7 1.8 collective-permute-start.8
  222.9 21.2 %collective-permute-done.8 = f32[512,512]{1,0:T(8,128)S(1)} collective-permute-done((f32[512,512]{1,0:T(8,128)S(1)}, f32[512,512]{1,0:T(8,128)S(1)}, u32[]{:S(2)}, u32[]{:S(2)}) %collective-permute-start.8) | collective-permute-done | bytes 1048608 | tf_op jit(solution)/shard_map/ppermute | solution.py:28
  247.8 2.3 collective-permute-start.11
  251.4 2.2 collective-permute-start.14
  253.5 2.6 collective-permute-start.15
  256.2 2.1 collective-permute-start.16
  259.5 4.0 %collective-permute-start.19 = (bf16[1,1,32,512]{3,2,1,0:T(8,128)(2,1)S(1)}, bf16[1,1,32,512]{3,2,1,0:T(8,128)(2,1)S(1)}, u32[]{:S(2)}, u32[]{:S(2)}) collective-permute-start(bf16[1,1,32,512]{3,2,1,0:T(8,128)(2,1)S(1)} %get-tuple-element.13), channel_id=1, source_target_pairs={{0,11},{1,12},{2,13},{3,14},{4,15},{5,0},{6,1},{7,2},{8,3},{9,4},{... | collective-permute-start | bytes 98312 | tf_op jit(solution)/shard_map/ppermute | solution.py:120
  264.2 2.5 collective-permute-start.22
  266.8 2.0 collective-permute-start.23
  268.8 1.5 collective-permute-done.23
  (89 shorter events, 22.9 us)
Async XLA Ops:
  0.7 18.8 %all-to-all-start = ((bf16[1,2,2,256,512]{4,3,2,0,1:T(8,128)(2,1)}), bf16[1,2,2,256,512]{4,3,2,0,1:T(8,128)(2,1)S(1)}, u32[]{:S(2)}, u32[]{:S(2)}) async-start(bf16[1,2,2,256,512]{4,3,2,0,1:T(8,128)(2,1)} %bitcast.92), calls=%async_computation | async-start | bytes 2097152 | tf_op jit(solution)/shard_map/all_to_all | solution.py:84
  82.3 2.7 %collective-permute-start = (f32[512,512]{1,0:T(8,128)S(1)}, f32[512,512]{1,0:T(8,128)S(1)}, u32[]{:S(2)}, u32[]{:S(2)}) collective-permute-start(f32[512,512]{1,0:T(8,128)S(1)} %fusion.24), channel_id=1, source_target_pairs={{0,1},{1,0},{2,3},{3,2},{4,5},{5,4},{6,7},{7,6},{8,9},{9,8},{10,11... | collective-permute-start | bytes 3145736 | tf_op jit(solution)/shard_map/ppermute | solution.py:28
  85.3 25.3 %collective-permute-start.1 = (f32[512,512]{1,0:T(8,128)S(1)}, f32[512,512]{1,0:T(8,128)S(1)}, u32[]{:S(2)}, u32[]{:S(2)}) collective-permute-start(f32[512,512]{1,0:T(8,128)S(1)} %add.238), channel_id=1, source_target_pairs={{0,2},{1,3},{2,0},{3,1},{4,6},{5,7},{6,4},{7,5},{8,10},{9,11},{10,... | collective-permute-start | bytes 3145736 | tf_op jit(solution)/shard_map/ppermute | solution.py:28
  110.8 24.7 %collective-permute-start.2 = (f32[512,512]{1,0:T(8,128)S(1)}, f32[512,512]{1,0:T(8,128)S(1)}, u32[]{:S(2)}, u32[]{:S(2)}) collective-permute-start(f32[512,512]{1,0:T(8,128)S(1)} %add.239), channel_id=1, source_target_pairs={{0,4},{1,5},{2,6},{3,7},{4,0},{5,1},{6,2},{7,3},{8,12},{9,13},{10,... | collective-permute-start | bytes 3145736 | tf_op jit(solution)/shard_map/ppermute | solution.py:28
  137.0 2.7 %collective-permute-start.3 = (f32[512,512]{1,0:T(8,128)S(1)}, f32[512,512]{1,0:T(8,128)S(1)}, u32[]{:S(2)}, u32[]{:S(2)}) collective-permute-start(f32[512,512]{1,0:T(8,128)S(1)} %fusion.25), channel_id=1, source_target_pairs={{0,1},{1,0},{2,3},{3,2},{4,5},{5,4},{6,7},{7,6},{8,9},{9,8},{10,11... | collective-permute-start | bytes 3145736 | tf_op jit(solution)/shard_map/ppermute | solution.py:28
  139.9 25.3 %collective-permute-start.4 = (f32[512,512]{1,0:T(8,128)S(1)}, f32[512,512]{1,0:T(8,128)S(1)}, u32[]{:S(2)}, u32[]{:S(2)}) collective-permute-start(f32[512,512]{1,0:T(8,128)S(1)} %add.243), channel_id=1, source_target_pairs={{0,2},{1,3},{2,0},{3,1},{4,6},{5,7},{6,4},{7,5},{8,10},{9,11},{10,... | collective-permute-start | bytes 3145736 | tf_op jit(solution)/shard_map/ppermute | solution.py:28
  165.4 24.4 %collective-permute-start.5 = (f32[512,512]{1,0:T(8,128)S(1)}, f32[512,512]{1,0:T(8,128)S(1)}, u32[]{:S(2)}, u32[]{:S(2)}) collective-permute-start(f32[512,512]{1,0:T(8,128)S(1)} %add.244), channel_id=1, source_target_pairs={{0,4},{1,5},{2,6},{3,7},{4,0},{5,1},{6,2},{7,3},{8,12},{9,13},{10,... | collective-permute-start | bytes 3145736 | tf_op jit(solution)/shard_map/ppermute | solution.py:28
  194.2 25.3 %collective-permute-start.7 = (f32[512,512]{1,0:T(8,128)S(1)}, f32[512,512]{1,0:T(8,128)S(1)}, u32[]{:S(2)}, u32[]{:S(2)}) collective-permute-start(f32[512,512]{1,0:T(8,128)S(1)} %add.248), channel_id=1, source_target_pairs={{0,2},{1,3},{2,0},{3,1},{4,6},{5,7},{6,4},{7,5},{8,10},{9,11},{10,... | collective-permute-start | bytes 3145736 | tf_op jit(solution)/shard_map/ppermute | solution.py:28
  219.7 24.4 %collective-permute-start.8 = (f32[512,512]{1,0:T(8,128)S(1)}, f32[512,512]{1,0:T(8,128)S(1)}, u32[]{:S(2)}, u32[]{:S(2)}) collective-permute-start(f32[512,512]{1,0:T(8,128)S(1)} %add.249), channel_id=1, source_target_pairs={{0,4},{1,5},{2,6},{3,7},{4,0},{5,1},{6,2},{7,3},{8,12},{9,13},{10,... | collective-permute-start | bytes 3145736 | tf_op jit(solution)/shard_map/ppermute | solution.py:28
  245.3 6.1 %collective-permute-start.9 = (bf16[1,1,32,512]{3,2,1,0:T(8,128)(2,1)S(1)}, bf16[1,1,32,512]{3,2,1,0:T(8,128)(2,1)S(1)}, u32[]{:S(2)}, u32[]{:S(2)}) collective-permute-start(bf16[1,1,32,512]{3,2,1,0:T(8,128)(2,1)S(1)} %get-tuple-element.23), channel_id=1, source_target_pairs={{0,1},{1,2},{2,3},{3,4},{4,5},{5,6},{6,7},{7,8},{8,9},{9,10},{10,1... | collective-permute-start | bytes 98312 | tf_op jit(solution)/shard_map/ppermute | solution.py:120
  246.5 7.0 %collective-permute-start.10 = (bf16[1,1,32,512]{3,2,1,0:T(8,128)(2,1)S(1)}, bf16[1,1,32,512]{3,2,1,0:T(8,128)(2,1)S(1)}, u32[]{:S(2)}, u32[]{:S(2)}) collective-permute-start(bf16[1,1,32,512]{3,2,1,0:T(8,128)(2,1)S(1)} %get-tuple-element.22), channel_id=1, source_target_pairs={{0,2},{1,3},{2,4},{3,5},{4,6},{5,7},{6,8},{7,9},{8,10},{9,11},{10,... | collective-permute-start | bytes 98312 | tf_op jit(solution)/shard_map/ppermute | solution.py:120
  247.8 8.4 %collective-permute-start.11 = (bf16[1,1,32,512]{3,2,1,0:T(8,128)(2,1)S(1)}, bf16[1,1,32,512]{3,2,1,0:T(8,128)(2,1)S(1)}, u32[]{:S(2)}, u32[]{:S(2)}) collective-permute-start(bf16[1,1,32,512]{3,2,1,0:T(8,128)(2,1)S(1)} %get-tuple-element.21), channel_id=1, source_target_pairs={{0,3},{1,4},{2,5},{3,6},{4,7},{5,8},{6,9},{7,10},{8,11},{9,12},{10... | collective-permute-start | bytes 98312 | tf_op jit(solution)/shard_map/ppermute | solution.py:120
  250.0 8.2 %collective-permute-start.12 = (bf16[1,1,32,512]{3,2,1,0:T(8,128)(2,1)S(1)}, bf16[1,1,32,512]{3,2,1,0:T(8,128)(2,1)S(1)}, u32[]{:S(2)}, u32[]{:S(2)}) collective-permute-start(bf16[1,1,32,512]{3,2,1,0:T(8,128)(2,1)S(1)} %get-tuple-element.20), channel_id=1, source_target_pairs={{0,4},{1,5},{2,6},{3,7},{4,8},{5,9},{6,10},{7,11},{8,12},{9,13},{1... | collective-permute-start | bytes 98312 | tf_op jit(solution)/shard_map/ppermute | solution.py:120
  250.7 7.6 %collective-permute-start.13 = (bf16[1,1,32,512]{3,2,1,0:T(8,128)(2,1)S(1)}, bf16[1,1,32,512]{3,2,1,0:T(8,128)(2,1)S(1)}, u32[]{:S(2)}, u32[]{:S(2)}) collective-permute-start(bf16[1,1,32,512]{3,2,1,0:T(8,128)(2,1)S(1)} %get-tuple-element.19), channel_id=1, source_target_pairs={{0,5},{1,6},{2,7},{3,8},{4,9},{5,10},{6,11},{7,12},{8,13},{9,14},{... | collective-permute-start | bytes 98312 | tf_op jit(solution)/shard_map/ppermute | solution.py:120
  251.4 8.1 %collective-permute-start.14 = (bf16[1,1,32,512]{3,2,1,0:T(8,128)(2,1)S(1)}, bf16[1,1,32,512]{3,2,1,0:T(8,128)(2,1)S(1)}, u32[]{:S(2)}, u32[]{:S(2)}) collective-permute-start(bf16[1,1,32,512]{3,2,1,0:T(8,128)(2,1)S(1)} %get-tuple-element.18), channel_id=1, source_target_pairs={{0,6},{1,7},{2,8},{3,9},{4,10},{5,11},{6,12},{7,13},{8,14},{9,15},... | collective-permute-start | bytes 98312 | tf_op jit(solution)/shard_map/ppermute | solution.py:120
  253.5 9.9 %collective-permute-start.15 = (bf16[1,1,32,512]{3,2,1,0:T(8,128)(2,1)S(1)}, bf16[1,1,32,512]{3,2,1,0:T(8,128)(2,1)S(1)}, u32[]{:S(2)}, u32[]{:S(2)}) collective-permute-start(bf16[1,1,32,512]{3,2,1,0:T(8,128)(2,1)S(1)} %get-tuple-element.17), channel_id=1, source_target_pairs={{0,7},{1,8},{2,9},{3,10},{4,11},{5,12},{6,13},{7,14},{8,15},{9,0},... | collective-permute-start | bytes 98312 | tf_op jit(solution)/shard_map/ppermute | solution.py:120
  256.2 7.8 %collective-permute-start.16 = (bf16[1,1,32,512]{3,2,1,0:T(8,128)(2,1)S(1)}, bf16[1,1,32,512]{3,2,1,0:T(8,128)(2,1)S(1)}, u32[]{:S(2)}, u32[]{:S(2)}) collective-permute-start(bf16[1,1,32,512]{3,2,1,0:T(8,128)(2,1)S(1)} %get-tuple-element.16), channel_id=1, source_target_pairs={{0,8},{1,9},{2,10},{3,11},{4,12},{5,13},{6,14},{7,15},{8,0},{9,1},... | collective-permute-start | bytes 98312 | tf_op jit(solution)/shard_map/ppermute | solution.py:120
  258.3 6.0 %collective-permute-start.17 = (bf16[1,1,32,512]{3,2,1,0:T(8,128)(2,1)S(1)}, bf16[1,1,32,512]{3,2,1,0:T(8,128)(2,1)S(1)}, u32[]{:S(2)}, u32[]{:S(2)}) collective-permute-start(bf16[1,1,32,512]{3,2,1,0:T(8,128)(2,1)S(1)} %get-tuple-element.15), channel_id=1, source_target_pairs={{0,9},{1,10},{2,11},{3,12},{4,13},{5,14},{6,15},{7,0},{8,1},{9,2},... | collective-permute-start | bytes 98312 | tf_op jit(solution)/shard_map/ppermute | solution.py:120
  258.3 8.5 %collective-permute-start.18 = (bf16[1,1,32,512]{3,2,1,0:T(8,128)(2,1)S(1)}, bf16[1,1,32,512]{3,2,1,0:T(8,128)(2,1)S(1)}, u32[]{:S(2)}, u32[]{:S(2)}) collective-permute-start(bf16[1,1,32,512]{3,2,1,0:T(8,128)(2,1)S(1)} %get-tuple-element.14), channel_id=1, source_target_pairs={{0,10},{1,11},{2,12},{3,13},{4,14},{5,15},{6,0},{7,1},{8,2},{9,3},... | collective-permute-start | bytes 98312 | tf_op jit(solution)/shard_map/ppermute | solution.py:120
  259.5 9.3 %collective-permute-start.19 = (bf16[1,1,32,512]{3,2,1,0:T(8,128)(2,1)S(1)}, bf16[1,1,32,512]{3,2,1,0:T(8,128)(2,1)S(1)}, u32[]{:S(2)}, u32[]{:S(2)}) collective-permute-start(bf16[1,1,32,512]{3,2,1,0:T(8,128)(2,1)S(1)} %get-tuple-element.13), channel_id=1, source_target_pairs={{0,11},{1,12},{2,13},{3,14},{4,15},{5,0},{6,1},{7,2},{8,3},{9,4},{... | collective-permute-start | bytes 98312 | tf_op jit(solution)/shard_map/ppermute | solution.py:120
  263.4 5.3 %collective-permute-start.20 = (bf16[1,1,32,512]{3,2,1,0:T(8,128)(2,1)S(1)}, bf16[1,1,32,512]{3,2,1,0:T(8,128)(2,1)S(1)}, u32[]{:S(2)}, u32[]{:S(2)}) collective-permute-start(bf16[1,1,32,512]{3,2,1,0:T(8,128)(2,1)S(1)} %get-tuple-element.12), channel_id=1, source_target_pairs={{0,12},{1,13},{2,14},{3,15},{4,0},{5,1},{6,2},{7,3},{8,4},{9,5},{1... | collective-permute-start | bytes 98312 | tf_op jit(solution)/shard_map/ppermute | solution.py:120
  264.0 4.8 %collective-permute-start.21 = (bf16[1,1,32,512]{3,2,1,0:T(8,128)(2,1)S(1)}, bf16[1,1,32,512]{3,2,1,0:T(8,128)(2,1)S(1)}, u32[]{:S(2)}, u32[]{:S(2)}) collective-permute-start(bf16[1,1,32,512]{3,2,1,0:T(8,128)(2,1)S(1)} %get-tuple-element.11), channel_id=1, source_target_pairs={{0,13},{1,14},{2,15},{3,0},{4,1},{5,2},{6,3},{7,4},{8,5},{9,6},{10... | collective-permute-start | bytes 98312 | tf_op jit(solution)/shard_map/ppermute | solution.py:120
  264.2 4.6 %collective-permute-start.22 = (bf16[1,1,32,512]{3,2,1,0:T(8,128)(2,1)S(1)}, bf16[1,1,32,512]{3,2,1,0:T(8,128)(2,1)S(1)}, u32[]{:S(2)}, u32[]{:S(2)}) collective-permute-start(bf16[1,1,32,512]{3,2,1,0:T(8,128)(2,1)S(1)} %get-tuple-element.10), channel_id=1, source_target_pairs={{0,14},{1,15},{2,0},{3,1},{4,2},{5,3},{6,4},{7,5},{8,6},{9,7},{10,... | collective-permute-start | bytes 98312 | tf_op jit(solution)/shard_map/ppermute | solution.py:120
  266.8 3.6 %collective-permute-start.23 = (bf16[1,1,32,512]{3,2,1,0:T(8,128)(2,1)S(1)}, bf16[1,1,32,512]{3,2,1,0:T(8,128)(2,1)S(1)}, u32[]{:S(2)}, u32[]{:S(2)}) collective-permute-start(bf16[1,1,32,512]{3,2,1,0:T(8,128)(2,1)S(1)} %get-tuple-element.9), channel_id=1, source_target_pairs={{0,15},{1,0},{2,1},{3,2},{4,3},{5,4},{6,5},{7,6},{8,7},{9,8},{10,9... | collective-permute-start | bytes 98312 | tf_op jit(solution)/shard_map/ppermute | solution.py:120
  (4 other events, 16.2 us)
